TPU v7x, 32 devices: a whole 2x2x4 slice. The times are simulated.
32 devices in a mesh: gx: 8 (over z, core), gy: 4 (over y, x).
Axes of the slice: x: 2, y: 2, z: 4, core: 2. Of those that a mesh axis runs over, the one named last changes fastest.
Arguments:
- hidden_in: bfloat16 [1024, 8192], P('gy', 'gx'), may hold values from -1200 to 1200
- norm_gain: bfloat16 [8192], P('gx'), may hold values from 0.099609375 to 1.8984375
- wq: bfloat16 [8192, 8192], P('gx', 'gy'), may hold values from -0.0625 to 0.0625
- wkv: bfloat16 [8192, 2, 1024], P('gx', None, 'gy'), may hold values from -0.125 to 0.125
- wo: bfloat16 [8192, 8192], P('gy', 'gx'), may hold values from -0.5 to 0.5
- kv_cache: bfloat16 [2, 8192, 1024], P(None, 'gx', 'gy'), may hold values from -200 to 200
- start: int32 [1], replicated, may hold values from 2048 to 8192
Outputs:
- attn_out: bfloat16 [1024, 8192], P('gy', 'gx')
All inputs are finite; a program needn't handle non-finite values.
Results may differ from a plain program's by a relative error of at most 0.009.
The roundings to bfloat16 on the way count: a program that leaves them out, or rounds other values in their place, can miss the bound.
Values may be sent and summed in bfloat16 or wider, within the bound.
A program may use at most 320 MiB of HBM per device.

v0:
```python
import math

import jax
import jax.numpy as jnp
from jax import lax
from jax.sharding import PartitionSpec as P

D = 8192
HD = 128


NEG_FILL = -1e30
EPSILON = 1e-05


def combine(former, latter):
    peak_former, totals_former, summed_former = former
    peak_latter, totals_latter, summed_latter = latter
    peak = jnp.maximum(peak_former, peak_latter)
    factor_former = jnp.exp(peak_former - peak)
    factor_latter = jnp.exp(peak_latter - peak)
    return (
        peak,
        totals_former * factor_former + totals_latter * factor_latter,
        summed_former * factor_former[..., None] + summed_latter * factor_latter[..., None],
    )


def block_terms(queries, query_pos, key_rows, value_rows, key_pos, key_live):
    score_scale = float(queries.shape[-1]) ** (-0.5)
    scores = (
        jnp.einsum("rgpe,lge->rgpl", queries, key_rows, preferred_element_type=jnp.float32)
        * score_scale
    )
    visible = (key_live[None, :] & (key_pos[None, :] <= query_pos[:, None]))[:, None, None, :]
    scores = jnp.where(visible, scores, NEG_FILL)
    peak = jnp.max(scores, axis=3)
    weights = jnp.where(visible, jnp.exp(scores - peak[..., None]), 0.0)
    totals = jnp.sum(weights, axis=3)
    summed = jnp.einsum(
        "rgpl,lge->rgpe",
        weights.astype(jnp.bfloat16),
        value_rows,
        preferred_element_type=jnp.float32,
    )
    return (peak, totals, summed)


def sweep_keys(running, queries, query_pos, key_rows, value_rows, key_pos, key_live, limit):
    length = key_rows.shape[0]
    stride = math.gcd(length, limit)
    amount = length // stride
    groups = key_rows.shape[1]
    blocks = (
        key_rows.reshape(amount, stride, groups, -1),
        value_rows.reshape(amount, stride, groups, -1),
        key_pos.reshape(amount, stride),
        key_live.reshape(amount, stride),
    )

    def advance(carried, block):
        return (combine(carried, block_terms(queries, query_pos, *block)), None)

    running, unused = lax.scan(advance, running, blocks)
    return running


def empty_state(amount, groups, per_group, head_size):
    return (
        jnp.full((amount, groups, per_group), NEG_FILL, jnp.float32),
        jnp.zeros((amount, groups, per_group), jnp.float32),
        jnp.zeros((amount, groups, per_group, head_size), jnp.float32),
    )


def local(hidden_in, norm_gain, wq, wkv, wo, kv_cache, start):
    anchor = start[0]
    rows_here = hidden_in.astype(jnp.float32)
    squares = lax.psum(jnp.sum(rows_here * rows_here, axis=1), "gx")
    scaled = (
        rows_here
        * lax.rsqrt(squares / D + EPSILON)[:, None]
        * norm_gain.astype(jnp.float32)[None, :]
    )
    normed_all = lax.all_gather(scaled.astype(jnp.bfloat16), "gy", axis=0, tiled=True)
    tokens = normed_all.shape[0]
    width_in = normed_all.shape[1]
    query_cols = wq.shape[1]
    key_cols = wkv.shape[2]
    groups = key_cols // HD
    per_group = query_cols // key_cols
    joined = jnp.concatenate([wq, wkv.reshape(width_in, 2 * key_cols)], axis=1)
    local_rows = tokens // lax.axis_size("gx")
    projected = lax.psum_scatter(
        jnp.dot(normed_all, joined, preferred_element_type=jnp.float32),
        "gx",
        scatter_dimension=0,
        tiled=True,
    ).astype(jnp.bfloat16)
    query_part = projected[:, :query_cols]
    recent = projected[:, query_cols:].reshape(local_rows, 2, key_cols)
    position = lax.axis_index("gx")
    recent_pos = anchor + position * local_rows + jnp.arange(local_rows, dtype=jnp.int32)
    queries = query_part.reshape(local_rows, groups, per_group, HD)
    portion = lax.all_gather(kv_cache, "gx", axis=1, tiled=True)
    length = portion.shape[1]
    slot_pos = jnp.arange(length, dtype=jnp.int32)
    running = sweep_keys(
        empty_state(local_rows, groups, per_group, HD),
        queries,
        recent_pos,
        portion[0].reshape(length, groups, HD),
        portion[1].reshape(length, groups, HD),
        slot_pos,
        slot_pos < anchor,
        2048,
    )
    portion = lax.all_gather(recent, "gx", axis=0, tiled=True)
    length = portion.shape[0]
    slot_pos = anchor + jnp.arange(length, dtype=jnp.int32)
    peak, totals, summed = sweep_keys(
        running,
        queries,
        recent_pos,
        portion[:, 0].reshape(length, groups, HD),
        portion[:, 1].reshape(length, groups, HD),
        slot_pos,
        jnp.ones((length,), jnp.bool_),
        2048,
    )
    local_heads = (summed / totals[..., None]).astype(jnp.bfloat16).reshape(local_rows, query_cols)
    attended = lax.all_gather(local_heads, "gx", axis=0, tiled=True)
    result = lax.psum_scatter(
        jnp.dot(attended, wo, preferred_element_type=jnp.float32),
        "gy",
        scatter_dimension=0,
        tiled=True,
    )
    return result.astype(jnp.bfloat16)


def solution(mesh):
    in_specs = (
        P("gy", "gx"),
        P("gx"),
        P("gx", "gy"),
        P("gx", None, "gy"),
        P("gy", "gx"),
        P(None, "gx", "gy"),
        P(),
    )
    out_specs = P("gy", "gx")
    return jax.shard_map(local, mesh=mesh, in_specs=in_specs, out_specs=out_specs, check_vma=False)
```

profile of v0, /device:TPU:0, one launch (start us, length us, event | category | flops | bytes accessed | tf_op | source)
XLA Modules:
  0.0 459.8 jit_solution(10663827329171784423)
XLA Ops:
  6.5 1.2 fusion.42
  7.8 18.1 %psum.7 = f32[256]{0:T(256)S(1)} all-reduce(f32[256]{0:T(256)S(1)} %fusion.42), channel_id=1, replica_groups=mesh['gx'=8,'gy'=4] {'gx'}, use_global_device_ids=true, to_apply=%region_1.0 | all-reduce | flops 256 | bytes 2048 | tf_op jit(solution)/shard_map/psum | solution.py:79
  25.8 0.7 convert_element_type.26
  26.5 2.0 fusion.44
  28.6 0.0 all-gather.5.cloned.1.call-start
  28.6 0.7 all-gather.5.cloned.1.call-update
  29.4 1.5 copy.32
  30.8 31.4 %all-gather.7.cloned.1.call-done = bf16[1024,1024]{1,0:T(8,128)(2,1)} async-done(((bf16[256,1024]{1,0:T(8,128)(2,1)}), bf16[1024,1024]{1,0:T(8,128)(2,1)}) %all-gather.7.cloned.1.call-update) | async-done | bytes 2097168 | tf_op jit(solution)/shard_map/all_gather | solution.py:85
  62.3 10.7 %fusion.26 = f32[1024,2560]{1,0:T(8,128)} fusion(bf16[1024,1024]{1,0:T(8,128)(2,1)} %all-gather.7.cloned.1.call-done, bf16[1024,512]{1,0:T(8,128)(2,1)S(1)} %bitcast.113, bf16[1024,2048]{1,0:T(8,128)(2,1)} %param.11), kind=kOutput, calls=%fused_computation.34 | convolution fusion | flops 5379194880 | bytes 17825792 | tf_op jit(solution)/shard_map/dot_general | solution.py:95
  73.0 0.0 all-gather.9.cloned.1.call-start
  73.8 0.6 multiply_add_fusion
  74.4 0.2 broadcast_compare_fusion
  74.6 71.4 %all-gather.5.cloned.1.call-done = bf16[2,8192,256]{2,1,0:T(8,128)(2,1)} async-done(((bf16[2,1024,256]{2,1,0:T(8,128)(2,1)}), bf16[2,8192,256]{2,1,0:T(8,128)(2,1)}) %all-gather.5.cloned.1.call-update) | async-done | bytes 8388624 | tf_op jit(solution)/shard_map/all_gather | solution.py:105
  146.0 5.9 %fusion.57 = (bf16[1,8192,256]{2,1,0:T(8,128)(2,1)}, bf16[1,8192,256]{2,1,0:T(8,128)(2,1)}) fusion(bf16[2,8192,256]{2,1,0:T(8,128)(2,1)} %all-gather.5.cloned.1.call-done), kind=kLoop, calls=%fused_computation.67 | loop fusion | bytes 16777216 | tf_op jit(solution)/shard_map/slice | solution.py:113
  151.9 7.1 %reshape_reshape_squeeze.9 = bf16[4,2048,2,128]{3,2,1,0:T(2,128)(2,1)} reshape(bf16[1,8192,256]{2,1,0:T(8,128)(2,1)} %get-tuple-element.176) | data formatting | bytes 8388608 | tf_op jit(solution)/shard_map/reshape;reshape;squeeze | solution.py:56
  158.9 6.9 %reshape_reshape_squeeze.8 = bf16[4,2048,2,128]{3,2,1,0:T(2,128)(2,1)} reshape(bf16[1,8192,256]{2,1,0:T(8,128)(2,1)} %get-tuple-element.177) | data formatting | bytes 8388608 | tf_op jit(solution)/shard_map/reshape;reshape;squeeze | solution.py:55
  165.9 90.4 %reduce-scatter.3.cloned.1.call-done = f32[128,2560]{1,0:T(8,128)} async-done(((f32[1024,2560]{1,0:T(8,128)}), f32[128,2560]{1,0:T(8,128)}) %reduce-scatter.3.cloned.1.call-update) | async-done | bytes 1310736 | tf_op jit(solution)/shard_map/reduce_scatter | solution.py:94
  256.2 1.4 convert_element_type.28
  257.7 0.1 copy.33
  257.8 0.8 copy.27
  258.6 0.2 all-gather.11.cloned.1.call-start
  258.8 0.1 copy.15
  259.0 76.3 %while.3 = (s32[]{:T(128)}, f32[128,2,8]{0,2,1:T(8,128)}, f32[128,2,8]{0,2,1:T(8,128)S(1)}, f32[128,2,8,128]{0,3,2,1:T(8,128)}, pred[4,2048]{1,0:T(4,128)(4,1)S(...) while((s32[]{:T(128)}, f32[128,2,8]{0,2,1:T(8,128)}, ...), condition=%wide.region_6.7_spmd.clone, body=%wide.region_3.6_spmd.clone.sunk | while | flops 2203594752 | bytes 75185440 | solution.py:64
  259.0 0.8 constant_dynamic-slice_fusion.5
  259.8 1.5 compare_and_fusion.2
  261.3 2.7 constant_dynamic-slice_fusion.6
  264.0 2.1 copy.45
  266.1 2.5 fusion.76
  268.6 4.0 fusion.77
  272.7 4.4 fusion.79
  277.1 1.0 copy-done.5
  278.1 0.8 constant_dynamic-slice_fusion.5
  278.9 1.5 compare_and_fusion.2
  280.4 2.7 constant_dynamic-slice_fusion.6
  283.1 2.1 copy.45
  285.2 2.5 fusion.76
  287.7 4.0 fusion.77
  291.8 4.4 fusion.79
  296.2 1.0 copy-done.5
  297.2 0.8 constant_dynamic-slice_fusion.5
  298.0 1.5 compare_and_fusion.2
  299.5 2.7 constant_dynamic-slice_fusion.6
  302.2 2.1 copy.45
  304.2 2.5 fusion.76
  306.8 4.0 fusion.77
  310.9 4.4 fusion.79
  315.2 1.0 copy-done.5
  316.3 0.8 constant_dynamic-slice_fusion.5
  317.0 1.5 compare_and_fusion.2
  318.5 2.7 constant_dynamic-slice_fusion.6
  321.2 2.1 copy.45
  323.3 2.5 fusion.76
  325.9 4.0 fusion.77
  329.9 4.4 fusion.79
  334.3 1.0 copy-done.5
  335.3 1.3 fusion.58
  336.6 1.5 fusion.23
  338.1 2.2 fusion.24
  340.4 3.0 divide_convert_fusion
  343.4 0.0 reduce-scatter.5.cloned.1.call-start
  343.5 46.3 %all-gather.11.cloned.1.call-done = bf16[1024,2048]{0,1:T(8,128)(2,1)} async-done(((bf16[128,2048]{0,1:T(8,128)(2,1)}), bf16[1024,2048]{0,1:T(8,128)(2,1)}) %all-gather.11.cloned.1.call-update) | async-done | bytes 4194320 | tf_op jit(solution)/shard_map/all_gather | solution.py:132
  389.8 10.0 %fusion.59 = f32[1024,1024]{1,0:T(8,128)} fusion(bf16[1024,2048]{0,1:T(8,128)(2,1)} %all-gather.11.cloned.1.call-done, bf16[2048,1024]{1,0:T(8,128)(2,1)} %param.13), kind=kOutput, calls=%fused_computation.69 | convolution fusion | flops 4294967296 | bytes 12582912 | tf_op jit(solution)/shard_map/dot_general | solution.py:134
  399.8 51.1 %reduce-scatter.5.cloned.1.call-done = f32[256,1024]{1,0:T(8,128)} async-done(((f32[1024,1024]{1,0:T(8,128)}), f32[256,1024]{1,0:T(8,128)}) %reduce-scatter.5.cloned.1.call-update) | async-done | bytes 1048592 | tf_op jit(solution)/shard_map/reduce_scatter | solution.py:133
  450.8 2.1 convert_element_type.31
  (70 shorter events, 0.6 us)
Async XLA Ops:
  6.5 55.7 %all-gather.7.cloned.1.call-start = ((), (), s32[]{:S(2)}) async-start(), calls=%async_computation.3 | async-start | bytes 2621440 | tf_op jit(solution)/shard_map/all_gather | solution.py:85
  28.6 117.4 %all-gather.5.cloned.1.call-start = ((), (), s32[]{:S(2)}) async-start(), calls=%async_computation.2 | async-start | bytes 9437184 | tf_op jit(solution)/shard_map/all_gather | solution.py:105
  29.3 226.9 %reduce-scatter.3.cloned.1.call-start = ((), (), s32[]{:S(2)}) async-start(), calls=%async_computation.4 | async-start | bytes 11796480 | tf_op jit(solution)/shard_map/reduce_scatter | solution.py:94
  73.0 262.4 %all-gather.9.cloned.1.call-start = ((), (), s32[]{:S(2)}) async-start(), calls=%async_computation.5 | async-start | bytes 1179648 | tf_op jit(solution)/shard_map/all_gather | solution.py:118
  258.6 131.1 %all-gather.11.cloned.1.call-start = ((), (), s32[]{:S(2)}) async-start(), calls=%async_computation.6 | async-start | bytes 4718592 | tf_op jit(solution)/shard_map/all_gather | solution.py:132
  268.6 4.0 copy-start.1
  268.6 4.1 copy-start
  268.6 4.1 copy-start.4
  272.7 4.4 copy-start.2
  277.1 1.0 copy-start.5
  287.7 4.0 copy-start.1
  287.7 4.1 copy-start
  287.7 4.1 copy-start.4
  291.8 4.4 copy-start.2
  296.2 1.0 copy-start.5
  306.8 4.0 copy-start.1
  306.8 4.1 copy-start
  306.8 4.1 copy-start.4
  310.8 4.4 copy-start.2
  315.2 1.0 copy-start.5
  325.8 4.0 copy-start.1
  325.8 4.1 copy-start
  325.9 4.1 copy-start.4
  329.9 4.4 copy-start.2
  334.3 1.0 copy-start.5
  336.6 3.8 copy-start.3
  336.6 3.8 copy-start.6
  343.4 107.4 %reduce-scatter.5.cloned.1.call-start = ((), (), s32[]{:S(2)}) async-start(), calls=%async_computation.7 | async-start | bytes 5242880 | tf_op jit(solution)/shard_map/reduce_scatter | solution.py:133
Sparse Core Ops, SparseCore 0:
  28.7 33.5 all-gather.6
  63.9 82.0 all-gather.4
  148.3 107.9 reduce-scatter.2
  258.7 22.3 all-gather.8
  343.6 46.1 all-gather.10
  399.9 50.9 reduce-scatter.4
where the time goes:
time: 461 us; the launch traced here: 460 us
  waiting for transfers between devices  291 us (63%)
  matrix products  52.7 us (11%)
  local copies, waits for them, and re-layouts  50 us (11%)
  other arithmetic  32.5 us (7%)
  blocking collectives  18.1 us (4%)
  between operations  14.3 us (3%)
    reduce_scatter x1, waiting for transfers between devices, local(): lax.psum_scatter(jnp.dot(normed_all, joined, preferred_element_type=jnp.f...  90.4 us
    all_gather x1, waiting for transfers between devices, local(): portion = lax.all_gather(kv_cache, 'gx', axis=1, tiled=True)  71.4 us
    reduce_scatter x1, waiting for transfers between devices, local(): lax.psum_scatter(jnp.dot(attended, wo, preferred_element_type=jnp.float32...  51.1 us
    all_gather x1, waiting for transfers between devices, local(): attended = lax.all_gather(local_heads, 'gx', axis=0, tiled=True)  46.3 us
    all_gather x1, waiting for transfers between devices, local(): lax.all_gather(scaled.astype(jnp.bfloat16), 'gy', axis=0, tiled=True)  31.4 us
    dynamic_slice x16, local copies, waits for them, and re-layouts, sweep_keys(): running, unused = lax.scan(advance, running, blocks)  22.3 us
    dot_general x5, matrix products, block_terms(): jnp.einsum('rgpl,lge->rgpe', weights.astype(jnp.bfloat16), value_rows, pr...  20.5 us
    reduce_sum x5, other arithmetic, block_terms(): totals = jnp.sum(weights, axis=3)  18.2 us
  transfers between devices with their start and end apart: 6, of which 5 were waited for; matrix products, arithmetic and copies ran while one was open for 23% of the time, Pallas kernels for 0%

commit v1 on v0

v1 whole, which is shorter than its diff:
```python
import functools
import math

import jax
import jax.numpy as jnp
from jax import lax
from jax.experimental import pallas as pl
from jax.experimental.pallas import tpu as pltpu
from jax.sharding import PartitionSpec as P

HD = 128
NEG_FILL = -1e30
EPSILON = 1e-05
LOG2E = 1.4426950408889634


def attention_kernel(heads_per_step, regions, info_ref, q_ref, *refs):
    caches = refs[:regions]
    fresh_ref, out_ref = refs[regions:]
    rows = q_ref.shape[0]
    pieces, _, length, _ = caches[0].shape
    scale = (HD ** -0.5) * LOG2E
    queries = [q_ref[:, h * HD : (h + 1) * HD] for h in range(heads_per_step)]

    def step(carried, keys, values, mask):
        result = []
        scores = [
            lax.dot_general(q, keys, (((1,), (1,)), ((), ())), preferred_element_type=jnp.float32)
            for q in queries
        ]
        for (peak, totals, summed), score in zip(carried, scores):
            if mask is not None:
                score = jnp.where(mask, score, NEG_FILL)
            higher = jnp.maximum(peak, jnp.max(score, axis=1, keepdims=True))
            weights = jnp.exp2((score - higher) * scale)
            factor = jnp.exp2((peak - higher) * scale)
            totals = totals * factor + jnp.sum(weights, axis=1, keepdims=True)
            summed = summed * factor + jnp.dot(
                weights.astype(jnp.bfloat16), values, preferred_element_type=jnp.float32
            )
            result.append((higher, totals, summed))
        return tuple(result)

    carried = tuple(
        (
            jnp.full((rows, 1), NEG_FILL, jnp.float32),
            jnp.zeros((rows, 1), jnp.float32),
            jnp.zeros((rows, HD), jnp.float32),
        )
        for _ in range(heads_per_step)
    )
    for region, cache in enumerate(caches):
        live = info_ref[region]
        full = live // length
        carried = lax.fori_loop(
            0, full, lambda j, c, cache=cache: step(c, cache[j, 0], cache[j, 1], None), carried
        )
        rest = live - full * length

        def tail(c, cache=cache, full=full, rest=rest):
            mask = lax.broadcasted_iota(jnp.int32, (rows, length), 1) < rest
            return step(c, cache[full, 0], cache[full, 1], mask)

        carried = lax.cond(rest > 0, tail, lambda c: c, carried)
    own = info_ref[regions]
    carried = lax.fori_loop(
        0, own, lambda j, c: step(c, fresh_ref[j, :, :HD], fresh_ref[j, :, HD:], None), carried
    )
    causal = lax.broadcasted_iota(jnp.int32, (rows, rows), 1) <= lax.broadcasted_iota(
        jnp.int32, (rows, rows), 0
    )
    carried = step(carried, fresh_ref[own, :, :HD], fresh_ref[own, :, HD:], causal)
    for h, (_, totals, summed) in enumerate(carried):
        out_ref[:, h * HD : (h + 1) * HD] = (summed / totals).astype(jnp.bfloat16)


def attention(info, queries, caches, fresh, heads_per_step=2):
    rows, cols = queries.shape
    heads = cols // HD
    width = heads_per_step * HD
    whole = lambda a: pl.BlockSpec(a.shape, lambda i, s, n=a.ndim: (0,) * n)
    return pl.pallas_call(
        functools.partial(attention_kernel, heads_per_step, len(caches)),
        out_shape=jax.ShapeDtypeStruct((rows, cols), jnp.bfloat16),
        grid_spec=pltpu.PrefetchScalarGridSpec(
            num_scalar_prefetch=1,
            grid=(heads // heads_per_step,),
            in_specs=[pl.BlockSpec((rows, width), lambda i, s: (0, i))]
            + [whole(c) for c in caches]
            + [whole(fresh)],
            out_specs=pl.BlockSpec((rows, width), lambda i, s: (0, i)),
        ),
        compiler_params=pltpu.CompilerParams(vmem_limit_bytes=50 * 1024 * 1024),
    )(info, queries, *caches, fresh)


def local(hidden_in, norm_gain, wq, wkv, wo, kv_cache, start):
    devices_x = lax.axis_size("gx")
    width_all = hidden_in.shape[1] * devices_x
    position = lax.axis_index("gx")
    groups = wkv.shape[2] // HD
    query_cols = wq.shape[1] // groups
    members = devices_x // groups
    part = position // members
    member = position % members
    teams = [[g * members + i for i in range(members)] for g in range(groups)]

    slots = kv_cache.shape[1]
    pieces = jnp.stack([kv_cache[:, :, g * HD : (g + 1) * HD] for g in range(groups)])
    caches = []
    live = []
    for shift in range(groups):
        source = (part + shift) % groups
        piece = pieces[(part - shift) % groups] if groups > 1 else pieces[0]
        if shift:
            pairs = [
                (j, ((j // members - shift) % groups) * members + j % members)
                for j in range(devices_x)
            ]
            piece = lax.ppermute(piece, "gx", pairs)
        caches.append(lax.all_gather(piece, "gx", axis=0, axis_index_groups=teams))
        span = members * slots
        live.append(jnp.clip(start[0] - source * span, 0, span))
    info = jnp.stack(live + [member]).astype(jnp.int32)

    own_rows = hidden_in.astype(jnp.float32)
    squares = lax.all_gather(jnp.sum(own_rows * own_rows, axis=1), ("gx", "gy"), axis=0)
    hidden = lax.all_gather(hidden_in, "gy", axis=0, tiled=True)
    tokens = hidden.shape[0]
    squares = jnp.sum(squares.reshape(devices_x, tokens), axis=0)
    normed = (
        hidden.astype(jnp.float32)
        * lax.rsqrt(squares / width_all + EPSILON)[:, None]
        * norm_gain.astype(jnp.float32)[None, :]
    ).astype(jnp.bfloat16)

    def project(weights):
        return jnp.dot(normed, weights, preferred_element_type=jnp.float32)

    width_in = wkv.shape[0]
    fresh = jnp.concatenate(
        [
            project(wkv[:, :, g * HD : (g + 1) * HD].reshape(width_in, 2 * HD))
            for g in range(groups)
        ]
    )
    fresh = lax.psum_scatter(fresh, "gx", scatter_dimension=0, tiled=True).astype(jnp.bfloat16)
    fresh = lax.all_gather(fresh, "gx", axis=0, axis_index_groups=teams)
    queries = jnp.concatenate(
        [project(wq[:, g * query_cols : (g + 1) * query_cols]) for g in range(groups)]
    )
    queries = lax.psum_scatter(queries, "gx", scatter_dimension=0, tiled=True).astype(jnp.bfloat16)

    heads = attention(info, queries, caches, fresh)

    heads = lax.all_gather(heads, "gx", axis=0, tiled=True).reshape(groups, tokens, query_cols)
    result = jnp.dot(heads[0], wo[:query_cols], preferred_element_type=jnp.float32)
    for g in range(1, groups):
        result += jnp.dot(
            heads[g],
            wo[g * query_cols : (g + 1) * query_cols],
            preferred_element_type=jnp.float32,
        )
    return lax.psum_scatter(
        result.astype(jnp.bfloat16), "gy", scatter_dimension=0, tiled=True
    )


def solution(mesh):
    in_specs = (
        P("gy", "gx"),
        P("gx"),
        P("gx", "gy"),
        P("gx", None, "gy"),
        P("gy", "gx"),
        P(None, "gx", "gy"),
        P(),
    )
    out_specs = P("gy", "gx")
    return jax.shard_map(local, mesh=mesh, in_specs=in_specs, out_specs=out_specs, check_vma=False)
```

time: 461 us -> 394 us (0.85)
  waiting for transfers between devices: 291 us -> 224 us
  blocking collectives: 18.1 us -> 80.3 us
  local copies, waits for them, and re-layouts: 50 us -> 5.66 us
  Pallas kernels: 0 us -> 36.5 us
  matrix products: 52.7 us -> 18.2 us
  other arithmetic: 32.5 us -> 11 us
    all_gather x4, waiting for transfers between devices: 149 us -> 54.4 us  [the longest x1 54.3 us: local(): lax.all_gather(heads, 'gx', axis=0, tiled=True)]
    all_gather x0 -> x2, blocking collectives: none -> 80.3 us  [the longest x1 69.7 us: local(): lax.all_gather(jnp.sum(own_rows * own_rows, axis=1), ('gx', 'gy'), axis=0)]
    pallas_call x0 -> x1, Pallas kernels: none -> 36.5 us  [attention(): pl.pallas_call(functools.partial(attention_kernel, heads_per_step, len(ca...]
    dot_general x12 -> x6, matrix products: 52.7 us -> 18.2 us  [the longest x4 9.79 us: project(): return jnp.dot(normed, weights, preferred_element_type=jnp.float32)]
    ppermute x0 -> x1, waiting for transfers between devices: none -> 27.1 us  [local(): piece = lax.ppermute(piece, 'gx', pairs)]
    dynamic_slice x16 -> x0, local copies, waits for them, and re-layouts: 22.3 us -> none  [sweep_keys(): running, unused = lax.scan(advance, running, blocks)]
    reduce_sum x6 -> x2, other arithmetic: 19.4 us -> 1.24 us  [the longest x1 1.22 us: local(): jnp.sum(own_rows * own_rows, axis=1)]
    psum x1 -> x0, blocking collectives: 18.1 us -> none  [local(): squares = lax.psum(jnp.sum(rows_here * rows_here, axis=1), 'gx')]
  transfers between devices with their start and end apart: 6 -> 8, of which waited for: 5 -> 5; matrix products, arithmetic and copies ran while one was open for 23% -> 5% of each run, Pallas kernels for 0% -> 0%
where the time goes in v1:
time: 394 us; the launch traced here: 392 us
  waiting for transfers between devices  224 us (57%)
  blocking collectives  80.3 us (20%)
  Pallas kernels  36.5 us (9%)
  matrix products  18.2 us (5%)
  between operations  15.5 us (4%)
  other arithmetic  11 us (3%)
  local copies, waits for them, and re-layouts  5.66 us (1%)
    reduce_scatter x1, waiting for transfers between devices, local(): lax.psum_scatter(queries, 'gx', scatter_dimension=0, tiled=True)  93.1 us
    all_gather x1, blocking collectives, local(): lax.all_gather(jnp.sum(own_rows * own_rows, axis=1), ('gx', 'gy'), axis=0)  69.7 us
    all_gather x1, waiting for transfers between devices, local(): lax.all_gather(heads, 'gx', axis=0, tiled=True)  54.3 us
    pallas_call x1, Pallas kernels, attention(): pl.pallas_call(functools.partial(attention_kernel, heads_per_step, len(ca...  36.5 us
    reduce_scatter x1, waiting for transfers between devices, local(): lax.psum_scatter(result.astype(jnp.bfloat16), 'gy', scatter_dimension=0,...  34.1 us
    ppermute x1, waiting for transfers between devices, local(): piece = lax.ppermute(piece, 'gx', pairs)  27.1 us
    reduce_scatter x1, waiting for transfers between devices, local(): lax.psum_scatter(fresh, 'gx', scatter_dimension=0, tiled=True)  15 us
    all_gather x1, blocking collectives, local(): fresh = lax.all_gather(fresh, 'gx', axis=0, axis_index_groups=teams)  10.6 us
  transfers between devices with their start and end apart: 8, of which 5 were waited for; matrix products, arithmetic and copies ran while one was open for 5% of the time, Pallas kernels for 0%

profile of v1, /device:TPU:0, one launch (start us, length us, event | category | flops | bytes accessed | tf_op | source)
XLA Modules:
  0.0 392.0 jit_solution(7216339927523091522)
XLA Ops:
  7.4 0.0 all-gather.9.cloned.1.call-start
  7.4 0.7 all-gather.9.cloned.1.call-update
  8.1 0.0 reduce-scatter.6.cloned.1.call-start
  8.1 0.7 convert_element_type.23
  8.8 1.2 multiply_reduce_fusion
  10.0 69.7 %all-gather.3 = f32[32,1,256]{2,1,0:T(1,128)S(1)} all-gather(f32[1,1,256]{2,1,0:T(1,128)S(1)} %bitcast.27), channel_id=2, replica_groups=mesh['gx'=8,'gy'=4] {'gx','gy'}, dimensions={0}, use_global_device_ids=true | all-gather | bytes 33792 | tf_op jit(solution)/shard_map/all_gather | solution.py:127
  79.8 0.1 reduce
  79.9 1.9 fusion.23
  81.8 0.0 all-gather.9.cloned.1.call-done
  81.9 0.0 copy-start.6
  81.9 2.5 fusion.17
  84.4 0.0 copy-done.6
  84.4 0.8 fusion.20
  85.2 1.5 pad_maximum_fusion.1
  86.6 0.0 reduce-scatter.6.cloned.1.call-update
  86.6 0.0 reduce-scatter.4.cloned.1.call-start
  86.7 0.0 copy-start.3
  86.7 4.1 %fusion.6 = f32[1024,1024]{1,0:T(8,128)S(1)} fusion(bf16[1024,2048]{1,0:T(8,128)(2,1)} %param.9, bf16[1024,1024]{1,0:T(8,128)(2,1)S(1)} %copy-done.6, f32[1024]{0:T(1024)S(1)} %convert_element_type.23, f32[1024]{0:T(1024)S(1)} %add_rsqrt_fusion), kind=kOutput, calls=%fused_computation.10 | convolution fusion | flops 2151677952 | bytes 8396800 | tf_op jit(solution)/shard_map/dot_general | solution.py:138
  90.8 0.0 copy-done.3
  90.8 2.4 fusion.8
  93.3 4.1 %pad_maximum_fusion = f32[2048,1024]{1,0:T(8,128)} fusion(f32[1024,1024]{1,0:T(8,128)S(1)} %fusion.6, f32[1024,1024]{1,0:T(8,128)S(1)} %fusion.8), kind=kLoop, calls=%fused_computation | loop fusion | flops 2097152 | bytes 16777216 | tf_op jit(solution)/shard_map/concatenate | solution.py:149
  97.3 0.0 copy-start.1
  97.3 0.0 reduce-scatter.4.cloned.1.call-update
  97.4 0.0 all-gather.11.cloned.1.call-start
  97.5 1.1 copy-done.1
  98.6 0.2 slice_bitcast_fusion
  98.7 1.2 fusion.15
  99.9 0.0 all-gather.11.cloned.1.call-update
  100.0 0.0 all-gather.15.cloned.1.call-start
  100.0 0.1 collective-permute-start
  100.1 27.1 %collective-permute-done = bf16[2,1024,128]{2,1,0:T(8,128)(2,1)S(1)} collective-permute-done((bf16[2,1024,128]{2,1,0:T(8,128)(2,1)S(1)}, bf16[2,1024,128]{2,1,0:T(8,128)(2,1)S(1)}, u32[]{:S(2)}, u32[]{:S(2)}) %collective-permute-start) | collective-permute-done | bytes 524320 | tf_op jit(solution)/shard_map/ppermute | solution.py:120
  127.2 0.0 copy-start.2
  127.2 0.8 copy-done.2
  128.1 0.0 all-gather.15.cloned.1.call-update
  128.1 0.0 all-gather.13.cloned.1.call-start
  128.8 0.1 pad_add_fusion.info_ref
  128.9 15.0 %reduce-scatter.6.cloned.1.call-done = f32[256,256]{1,0:T(8,128)} async-done(((f32[2048,256]{1,0:T(8,128)}), f32[256,256]{1,0:T(8,128)}) %reduce-scatter.6.cloned.1.call-update) | async-done | bytes 262160 | tf_op jit(solution)/shard_map/reduce_scatter | solution.py:147
  143.9 1.0 convert_element_type.26
  144.9 10.6 %all-gather.2 = bf16[1024,256]{1,0:T(8,128)(2,1)S(1)} all-gather(bf16[256,256]{1,0:T(8,128)(2,1)S(1)} %convert_element_type.26), channel_id=4, replica_groups={{0,4,8,12},{16,20,24,28},{1,5,9,13},{17,21,25,29},{2,6,10,14},{18,22,26..., dimensions={0}, use_global_device_ids=true | all-gather | bytes 655360 | tf_op jit(solution)/shard_map/all_gather | solution.py:148
  155.4 93.1 %reduce-scatter.4.cloned.1.call-done = f32[256,1024]{1,0:T(8,128)} async-done(((f32[2048,1024]{1,0:T(8,128)}), f32[256,1024]{1,0:T(8,128)}) %reduce-scatter.4.cloned.1.call-update) | async-done | bytes 1048592 | tf_op jit(solution)/shard_map/reduce_scatter | solution.py:152
  248.5 1.3 convert_element_type.25.q_ref
  249.8 0.0 all-gather.11.cloned.1.call-done.refs_0_
  249.8 0.0 all-gather.15.cloned.1.call-done
  249.8 0.0 copy-start
  249.9 1.6 copy-done
  251.4 36.5 %shard_map.73 = bf16[256,1024]{1,0:T(8,128)(2,1)} custom-call(s32[3]{0:T(128)S(1)} %pad_add_fusion.info_ref, bf16[256,1024]{1,0:T(8,128)(2,1)S(1)} %convert_element_type.25.q_ref, bf16[4,2,1024,128]{3,2,1,0:T(8,128)(2,1)S(1)} %copy-done, bf16[4,2,1024,128]{3,2,1,0:T(8,128)(2,1)} %bitcast.24, bf16[4,256,256]{2,1,0:T(8,128)(2,1)S(1)} %bitcast.23), custom_call_target="tpu_custom_call" | custom-call | tf_op jit(solution)/shard_map/pallas_call | solution.py:82
  288.0 0.0 all-gather.13.cloned.1.call-update
  288.0 0.0 reduce-scatter.8.cloned.1.call-start
  288.0 54.3 %all-gather.13.cloned.1.call-done = bf16[2048,1024]{1,0:T(8,128)(2,1)} async-done(((bf16[256,1024]{1,0:T(8,128)(2,1)}), bf16[2048,1024]{1,0:T(8,128)(2,1)}) %all-gather.13.cloned.1.call-update) | async-done | bytes 4194320 | tf_op jit(solution)/shard_map/all_gather | solution.py:156
  342.4 0.0 copy-start.4
  342.4 0.0 copy-start.5
  342.4 4.7 %fusion = f32[1024,1024]{1,0:T(8,128)S(1)} fusion(bf16[2048,1024]{1,0:T(8,128)(2,1)} %all-gather.13.cloned.1.call-done, bf16[2048,1024]{1,0:T(8,128)(2,1)} %param.11), kind=kOutput, calls=%fused_computation.3 | convolution fusion | flops 2147483648 | bytes 8388608 | tf_op jit(solution)/shard_map/dot_general | solution.py:159
  347.1 0.0 copy-done.4
  347.1 0.0 copy-done.5
  347.1 3.7 add_convert_fusion
  350.8 0.0 reduce-scatter.8.cloned.1.call-update
  350.8 34.1 %reduce-scatter.8.cloned.1.call-done = bf16[256,1024]{1,0:T(8,128)(2,1)} async-done(((bf16[1024,1024]{1,0:T(8,128)(2,1)}), bf16[256,1024]{1,0:T(8,128)(2,1)}) %reduce-scatter.8.cloned.1.call-update) | async-done | bytes 524304 | tf_op jit(solution)/shard_map/reduce_scatter | solution.py:164
  (3 shorter events, 0.0 us)
Async XLA Ops:
  7.4 74.5 %all-gather.9.cloned.1.call-start = ((), (), s32[]{:S(2)}) async-start(), calls=%async_computation.3 | async-start | bytes 2621440 | tf_op jit(solution)/shard_map/all_gather | solution.py:128
  8.1 135.8 %reduce-scatter.6.cloned.1.call-start = ((), (), s32[]{:S(2)}) async-start(), calls=%async_computation.6 | async-start | bytes 2359296 | tf_op jit(solution)/shard_map/reduce_scatter | solution.py:147
  81.9 2.5 copy-start.6
  86.6 161.8 %reduce-scatter.4.cloned.1.call-start = ((), (), s32[]{:S(2)}) async-start(), calls=%async_computation.4 | async-start | bytes 9437184 | tf_op jit(solution)/shard_map/reduce_scatter | solution.py:152
  86.7 4.1 %copy-start.3 = (bf16[1024,2048]{1,0:T(8,128)(2,1)S(1)}, bf16[1024,2048]{1,0:T(8,128)(2,1)}, u32[]{:S(2)}) copy-start(bf16[1024,2048]{1,0:T(8,128)(2,1)} %param.9) | copy-start | bytes 12582916
  97.3 1.2 copy-start.1
  97.4 152.5 %all-gather.11.cloned.1.call-start = ((), (), s32[]{:S(2)}) async-start(), calls=%async_computation.5 | async-start | bytes 2621440 | tf_op jit(solution)/shard_map/all_gather | solution.py:121
  100.0 149.9 %all-gather.15.cloned.1.call-start = ((), (), s32[]{:S(2)}) async-start(), calls=%async_computation.9 | async-start | bytes 2621440 | tf_op jit(solution)/shard_map/all_gather | solution.py:121
  100.0 27.2 %collective-permute-start = (bf16[2,1024,128]{2,1,0:T(8,128)(2,1)S(1)}, bf16[2,1024,128]{2,1,0:T(8,128)(2,1)S(1)}, u32[]{:S(2)}, u32[]{:S(2)}) collective-permute-start(bf16[2,1024,128]{2,1,0:T(8,128)(2,1)S(1)} %get-tuple-element.7), channel_id=1, source_target_pairs={{0,16},{4,20},{8,24},{12,28},{16,0},{20,4},{24,8},{28,12},{1,17},{... | collective-permute-start | bytes 1572872 | tf_op jit(solution)/shard_map/ppermute | solution.py:120
  127.2 0.8 copy-start.2
  128.1 214.3 %all-gather.13.cloned.1.call-start = ((), (), s32[]{:S(2)}) async-start(), calls=%async_computation.7 | async-start | bytes 4718592 | tf_op jit(solution)/shard_map/all_gather | solution.py:156
  249.8 1.6 copy-start
  288.0 96.9 %reduce-scatter.8.cloned.1.call-start = ((), (), s32[]{:S(2)}) async-start(), calls=%async_computation.8 | async-start | bytes 2621440 | tf_op jit(solution)/shard_map/reduce_scatter | solution.py:164
  342.4 4.7 %copy-start.4 = (bf16[2048,1024]{1,0:T(8,128)(2,1)S(1)}, bf16[2048,1024]{1,0:T(8,128)(2,1)}, u32[]{:S(2)}) copy-start(bf16[2048,1024]{1,0:T(8,128)(2,1)} %param.11) | copy-start | bytes 12582916
  342.4 4.7 %copy-start.5 = (bf16[2048,1024]{1,0:T(8,128)(2,1)S(1)}, bf16[2048,1024]{1,0:T(8,128)(2,1)}, u32[]{:S(2)}) copy-start(bf16[2048,1024]{1,0:T(8,128)(2,1)} %all-gather.13.cloned.1.call-done) | copy-start | bytes 12582916
Sparse Core Ops, SparseCore 0:
  10.0 38.1 all-gather.8
  86.8 57.0 reduce-scatter.5
  146.2 102.2 reduce-scatter.3
  288.1 54.2 all-gather.12
  350.9 33.9 reduce-scatter.7
Sparse Core Ops, SparseCore 1:
  100.0 37.6 all-gather.10
  139.1 44.7 all-gather.14
